TPU v7x, 128 devices: a whole 4x4x4 slice. The times are simulated.
128 devices in a mesh: dp: 4 (over x_hi, core), patch: 32 (over y, x_lo, z).
Axes of the slice: x: 4 (x_hi: 2, x_lo: 2; x = x_hi * 2 + x_lo), y: 4, z: 4, core: 2. Of those that a mesh axis runs over, the one named last changes fastest.
Arguments:
- query_tokens: bfloat16 [4, 64, 128, 768], P('dp', 'patch')
- past_tokens: bfloat16 [4, 256, 128, 768], P('dp', 'patch'), may hold values from -6 to 6
- source_dev: int32 [64, 4, 3], replicated, may hold values from 0 to 31, all different within a row; in each aligned block of 8 rows (0 to 7, 8 to 15, ..., all dimensions but the last counted through in order) at most 2 rows name the same one
- source_slot: int32 [64, 4, 3], replicated, may hold values from 0 to 7
- kept: int32 [64, 4, 3], replicated, may hold values 0 or 1
- w_query: bfloat16 [768, 768], replicated
- w_key: bfloat16 [768, 768], replicated
- w_value: bfloat16 [768, 768], replicated, may hold values from -0.21875 to 0.21875
- w_out: bfloat16 [768, 768], replicated, may hold values from -0.875 to 0.875
- grad_out: bfloat16 [4, 64, 128, 768], P('dp', 'patch'), may hold values from -6 to 6
Outputs:
- attn_out: bfloat16 [4, 64, 128, 768], P('dp', 'patch')
- grad_query_tokens: bfloat16 [4, 64, 128, 768], P('dp', 'patch')
- grad_past_tokens: bfloat16 [4, 256, 128, 768], P('dp', 'patch')
- grad_w_query: float32 [768, 768], replicated
- grad_w_key: float32 [768, 768], replicated
- grad_w_value: float32 [768, 768], replicated
- grad_w_out: float32 [768, 768], replicated
Inputs may be any that keep to these rules, and one draw needn't show every extreme that they name: `source_dev`: row (p, f) lists the devices holding the frame-f blocks that patch p reads: 3 different devices a row. Over the rows of one device's 2 patches, no device is listed more than 2 times, and some device is listed exactly 2 times.
All inputs are finite; a program needn't handle non-finite values.
Results may differ from a plain program's by a relative error of at most 0.013.
The roundings to bfloat16 on the way count: a program that leaves them out, or rounds other values in their place, can miss the bound.
Values may be sent and summed in bfloat16 or wider, within the bound.
A program may use at most 256 MiB of HBM per device.

v0:
```python
import math
import jax
import jax.numpy as jnp
from jax import lax
from jax.sharding import PartitionSpec as P

H = 12
HD = 64


def attend(queries, keys, values, live):
    groups, query_rows, model_width = queries.shape
    key_rows = keys.shape[1]
    inv_scale = 1.0 / math.sqrt(HD)
    head_query = queries.reshape(groups, query_rows, H, HD)
    head_key = keys.reshape(groups, key_rows, H, HD)
    head_value = values.reshape(groups, key_rows, H, HD)
    scores = (
        jnp.einsum("gqhe,gkhe->ghqk", head_query, head_key, preferred_element_type=jnp.float32)
        * inv_scale
    )
    scores = jnp.where(live[:, None, None, :] > 0, scores, -jnp.inf)
    row_max = jnp.max(scores, axis=-1, keepdims=True)
    shifted = jnp.exp(scores - row_max)
    soft_probs = shifted / jnp.sum(shifted, axis=-1, keepdims=True)
    soft_weights = soft_probs.astype(jnp.bfloat16)
    mixed = jnp.einsum(
        "ghqk,gkhe->gqhe", soft_weights, head_value, preferred_element_type=jnp.float32
    )
    mixed = mixed.reshape(groups, query_rows, model_width).astype(jnp.bfloat16)
    return (mixed, soft_probs, soft_weights)


def attend_back(queries, keys, values, soft_probs, soft_weights, upstream):
    groups, query_rows, model_width = queries.shape
    key_rows = keys.shape[1]
    inv_scale = 1.0 / math.sqrt(HD)
    head_query = queries.reshape(groups, query_rows, H, HD)
    head_key = keys.reshape(groups, key_rows, H, HD)
    head_value = values.reshape(groups, key_rows, H, HD)
    head_up = upstream.reshape(groups, query_rows, H, HD)
    grad_prob = jnp.einsum(
        "gqhe,gkhe->ghqk", head_up, head_value, preferred_element_type=jnp.float32
    )
    row_delta = jnp.sum(soft_probs * grad_prob, axis=-1, keepdims=True)
    grad_score = (soft_probs * (grad_prob - row_delta) * inv_scale).astype(jnp.bfloat16)
    grad_q = jnp.einsum("ghqk,gkhe->gqhe", grad_score, head_key, preferred_element_type=jnp.float32)
    grad_k = jnp.einsum(
        "ghqk,gqhe->gkhe", grad_score, head_query, preferred_element_type=jnp.float32
    )
    grad_v = jnp.einsum(
        "ghqk,gqhe->gkhe", soft_weights, head_up, preferred_element_type=jnp.float32
    )
    grad_q = grad_q.reshape(groups, query_rows, model_width).astype(jnp.bfloat16)
    grad_k = grad_k.reshape(groups, key_rows, model_width).astype(jnp.bfloat16)
    grad_v = grad_v.reshape(groups, key_rows, model_width).astype(jnp.bfloat16)
    return (grad_q, grad_k, grad_v)


def forward_group(inputs):
    queries, keys, values, live = inputs
    mixed, soft_probs, soft_weights = attend(queries[None], keys[None], values[None], live[None])
    return (mixed[0], soft_probs[0], soft_weights[0])


def backward_group(inputs):
    queries, keys, values, soft_probs, soft_weights, upstream = inputs
    grad_q, grad_k, grad_v = attend_back(
        queries[None],
        keys[None],
        values[None],
        soft_probs[None],
        soft_weights[None],
        upstream[None],
    )
    return (grad_q[0], grad_k[0], grad_v[0])


def transpose_dot(left, right):
    return jnp.einsum("nd,ed->ne", left, right, preferred_element_type=jnp.float32)


def outer_sum(left, right):
    return jnp.einsum("nd,ne->de", left, right, preferred_element_type=jnp.float32)


def body(
    query_tokens,
    past_tokens,
    source_dev,
    source_slot,
    kept,
    w_query,
    w_key,
    w_value,
    w_out,
    grad_out,
):
    batch_local, patch_local, block_rows, model_width = query_tokens.shape
    slots_local = past_tokens.shape[1]
    peer_count = lax.axis_size("patch")
    device = lax.axis_index("patch")
    requests = source_dev.shape[1] * source_dev.shape[2]
    per_device = patch_local * requests
    capacity = max(2, (per_device + peer_count - 1) // peer_count + 1)
    owners = source_dev.reshape(peer_count, per_device)
    places = source_slot.reshape(peer_count, per_device)
    live_all = kept.reshape(peer_count, per_device)
    request_order = jnp.arange(per_device)
    earlier = request_order[:, None] > request_order[None, :]
    matches = (owners[:, :, None] == owners[:, None, :]) & earlier[None]
    slot_rank = jnp.sum(matches.astype(jnp.int32), axis=2)
    from_here = (owners == device) & (live_all > 0)
    slot_hit = (slot_rank[:, :, None] == jnp.arange(capacity)[None, None, :]) & from_here[
        :, :, None
    ]
    place_hit = places[:, :, None] == jnp.arange(slots_local)[None, None, :]
    chooser = jnp.einsum(
        "dqc,dqs->dcs", slot_hit.astype(jnp.float32), place_hit.astype(jnp.float32)
    ).astype(jnp.bfloat16)
    outgoing = jnp.einsum(
        "dcs,bsnw->bdcnw", chooser, past_tokens, preferred_element_type=jnp.float32
    ).astype(jnp.bfloat16)
    incoming = lax.all_to_all(outgoing, "patch", split_axis=1, concat_axis=1, tiled=True)
    my_owner = lax.dynamic_index_in_dim(owners, device, 0, keepdims=False)
    my_rank = lax.dynamic_index_in_dim(slot_rank, device, 0, keepdims=False)
    my_live = lax.dynamic_index_in_dim(live_all, device, 0, keepdims=False)
    position = my_owner * capacity + my_rank
    arrived = incoming.reshape(batch_local, peer_count * capacity, block_rows, model_width)
    fetched = jnp.take(arrived, position, axis=1)
    fetched_rows = fetched.reshape(batch_local * per_device * block_rows, model_width)
    w_proj = jnp.concatenate([w_query, w_key, w_value], axis=1)
    w_pair = jnp.concatenate([w_key, w_value], axis=1)
    token_rows = query_tokens.reshape(-1, model_width)
    own_proj = jnp.dot(token_rows, w_proj, preferred_element_type=jnp.float32).astype(jnp.bfloat16)
    far_proj = jnp.dot(fetched_rows, w_pair, preferred_element_type=jnp.float32).astype(
        jnp.bfloat16
    )
    groups = batch_local * patch_local
    far_rows = requests * block_rows
    queries = own_proj[:, :model_width].reshape(groups, block_rows, model_width)
    all_keys = jnp.concatenate(
        [
            own_proj[:, model_width : 2 * model_width].reshape(groups, block_rows, model_width),
            far_proj[:, :model_width].reshape(groups, far_rows, model_width),
        ],
        axis=1,
    )
    all_values = jnp.concatenate(
        [
            own_proj[:, 2 * model_width :].reshape(groups, block_rows, model_width),
            far_proj[:, model_width:].reshape(groups, far_rows, model_width),
        ],
        axis=1,
    )
    live_far = jnp.repeat(my_live.reshape(patch_local, requests), block_rows, axis=1)
    live_row = jnp.concatenate([jnp.ones((patch_local, block_rows), jnp.int32), live_far], axis=1)
    live_row = jnp.tile(live_row, (batch_local, 1))
    mixed, soft_probs, soft_weights = lax.map(
        forward_group, (queries, all_keys, all_values, live_row)
    )
    mixed_rows = mixed.reshape(-1, model_width)
    result = jnp.dot(mixed_rows, w_out, preferred_element_type=jnp.float32).astype(jnp.bfloat16)
    grad_rows = grad_out.reshape(-1, model_width)
    upstream = transpose_dot(grad_rows, w_out).astype(jnp.bfloat16)
    grad_wo = outer_sum(mixed_rows, grad_rows)
    grad_q, grad_k, grad_v = lax.map(
        backward_group,
        (
            queries,
            all_keys,
            all_values,
            soft_probs,
            soft_weights,
            upstream.reshape(groups, block_rows, model_width),
        ),
    )
    q_rows = grad_q.reshape(-1, model_width)
    own_k = grad_k[:, :block_rows].reshape(-1, model_width)
    own_v = grad_v[:, :block_rows].reshape(-1, model_width)
    far_k = grad_k[:, block_rows:].reshape(-1, model_width)
    far_v = grad_v[:, block_rows:].reshape(-1, model_width)
    grad_tokens = (
        transpose_dot(q_rows, w_query) + transpose_dot(own_k, w_key) + transpose_dot(own_v, w_value)
    ).astype(jnp.bfloat16)
    far_grad = (transpose_dot(far_k, w_key) + transpose_dot(far_v, w_value)).astype(jnp.bfloat16)
    far_grad = far_grad.reshape(batch_local, per_device, block_rows, model_width)
    back_rows = jnp.zeros(
        (batch_local, peer_count * capacity, block_rows, model_width), jnp.bfloat16
    )
    back_rows = back_rows.at[:, position].set(far_grad)
    returned = lax.all_to_all(
        back_rows.reshape(batch_local, peer_count, capacity, block_rows, model_width),
        "patch",
        split_axis=1,
        concat_axis=1,
        tiled=True,
    )
    past_grad = jnp.einsum(
        "dcs,bdcnw->bsnw", chooser, returned, preferred_element_type=jnp.float32
    ).astype(jnp.bfloat16)
    grad_wq = outer_sum(token_rows, q_rows)
    grad_wk = outer_sum(token_rows, own_k) + outer_sum(fetched_rows, far_k)
    grad_wv = outer_sum(token_rows, own_v) + outer_sum(fetched_rows, far_v)
    grad_wq, grad_wk, grad_wv, grad_wo = lax.psum(
        (grad_wq, grad_wk, grad_wv, grad_wo), ("dp", "patch")
    )
    inv_total = 1.0 / math.sqrt(
        lax.axis_size("dp") * batch_local * peer_count * patch_local * block_rows
    )
    return (
        result.reshape(query_tokens.shape),
        grad_tokens.reshape(query_tokens.shape),
        past_grad,
        grad_wq * inv_total,
        grad_wk * inv_total,
        grad_wv * inv_total,
        grad_wo * inv_total,
    )


def solution(mesh):
    placed = (
        P("dp", "patch", None, None),
        P("dp", "patch", None, None),
        P(),
        P(),
        P(),
        P(),
        P(),
        P(),
        P(),
        P("dp", "patch", None, None),
    )
    return jax.shard_map(
        body,
        mesh=mesh,
        in_specs=placed,
        out_specs=(
            P("dp", "patch", None, None),
            P("dp", "patch", None, None),
            P("dp", "patch", None, None),
            P(),
            P(),
            P(),
            P(),
        ),
        check_vma=False,
    )
```

profile of v0, /device:TPU:1, one launch (start us, length us, event | category | flops | bytes accessed | tf_op | source)
XLA Modules:
  0.0 947.2 jit_solution(16771115224350771100)
XLA Ops:
  10.7 5.1 convert_bitcast_fusion
  15.9 21.9 %copy.171 = bf16[1,32,2,128,768]{4,3,2,0,1:T(8,128)(2,1)} copy(bf16[1,32,2,128,768]{4,1,3,2,0:T(8,128)(2,1)S(1)} %convert_bitcast_fusion) | data formatting | bytes 25165824 | tf_op jit(solution)/shard_map/convert_element_type | solution.py:123
  37.8 10.3 %all-to-all-start = ((bf16[1,32,2,128,768]{4,3,2,0,1:T(8,128)(2,1)}), bf16[1,32,2,128,768]{4,3,2,0,1:T(8,128)(2,1)}, u32[]{:S(2)}, u32[]{:S(2)}) async-start(bf16[1,32,2,128,768]{4,3,2,0,1:T(8,128)(2,1)} %copy.171), calls=%async_computation | async-start | bytes 25165824 | tf_op jit(solution)/shard_map/all_to_all | solution.py:124
  48.2 2.7 fusion.24
  55.1 223.6 %all-to-all-done = bf16[1,32,2,128,768]{4,3,2,0,1:T(8,128)(2,1)} async-done(((bf16[1,32,2,128,768]{4,3,2,0,1:T(8,128)(2,1)}), bf16[1,32,2,128,768]{4,3,2,0,1:T(8,128)(2,1)}, u32[]{:S(2)}, u32[]{:S(2)}) %all-to-all-start) | async-done | bytes 12582944 | tf_op jit(solution)/shard_map/all_to_all | solution.py:124
  278.6 7.7 gather_fusion
  286.3 3.4 bitcast_select_fusion.1
  289.7 9.9 %convolution_convert_fusion.3 = bf16[3072,1536]{1,0:T(8,128)(2,1)} fusion(bf16[3072,768]{1,0:T(8,128)(2,1)S(1)} %bitcast_select_fusion.1, bf16[768,768]{1,0:T(8,128)(2,1)S(1)} %copy-done.16, bf16[768,768]{1,0:T(8,128)(2,1)S(1)} %copy-done.13), kind=kOutput, calls=%fused_computation.46 | convolution fusion | flops 7257194496 | bytes 16515072 | tf_op jit(solution)/shard_map/dot_general | solution.py:136
  299.6 7.9 fusion.56
  307.5 6.7 copy.173
  314.2 6.8 copy.175
  321.0 8.5 pad_maximum_fusion
  329.6 73.8 %while.28 = (s32[]{:T(128)}, bf16[2,128,768]{2,1,0:T(8,128)(2,1)S(1)}, f32[2,12,128,1664]{3,2,1,0:T(8,128)}, bf16[2,12,128,1664]{3,2,1,0:T(8,128)(2,1)}, bf16[2,...) while((s32[]{:T(128)}, ...), condition=%wide.region_4.5_spmd, body=%wide.region_1.0_spmd.sunk | while | flops 672304384 | bytes 83390360 | solution.py:159
  330.1 5.1 constant_dynamic-slice_fusion.14
  335.3 8.5 fusion.124
  343.8 9.6 %bitcast_dynamic-update-slice_fusion.4 = (bf16[2,12,128,1664]{3,2,1,0:T(8,128)(2,1)}, bf16[12,128,1664]{2,1,0:T(8,128)(2,1)}) fusion(bf16[2,12,128,1664]{3,2,1,0:T(8,128)(2,1)} %get-tuple-element.460, s32[]{:T(128)S(6)} %copy.244, f32[12,128,1664]{2,1,0:T(8,128)} %get-tuple-element.430, f32[12,128]{1,0:T(8,128)S(1)} %get-tuple-element.431), kind=kLoop, calls=%fused_computation.27.clone.1 | loop fusion | flops 5111808 | bytes 20453380 | tf_op jit(solution)/shard_map/while/body/jit(dynamic_update_index_in_dim)/dynamic_update_slice | solution.py:159
  353.4 4.4 convolution_convert_fusion.10
  358.0 8.8 bitcast_dynamic-update-slice_fusion.5
  366.8 5.1 constant_dynamic-slice_fusion.14
  372.0 8.5 fusion.124
  380.5 9.6 %bitcast_dynamic-update-slice_fusion.4 = (bf16[2,12,128,1664]{3,2,1,0:T(8,128)(2,1)}, bf16[12,128,1664]{2,1,0:T(8,128)(2,1)}) fusion(bf16[2,12,128,1664]{3,2,1,0:T(8,128)(2,1)} %get-tuple-element.460, s32[]{:T(128)S(6)} %copy.244, f32[12,128,1664]{2,1,0:T(8,128)} %get-tuple-element.430, f32[12,128]{1,0:T(8,128)S(1)} %get-tuple-element.431), kind=kLoop, calls=%fused_computation.27.clone.1 | loop fusion | flops 5111808 | bytes 20453380 | tf_op jit(solution)/shard_map/while/body/jit(dynamic_update_index_in_dim)/dynamic_update_slice | solution.py:159
  390.1 4.4 convolution_convert_fusion.10
  394.7 8.7 bitcast_dynamic-update-slice_fusion.5
  404.1 108.9 %while.29 = (s32[]{:T(128)}, bf16[2,128,768]{2,1,0:T(8,128)(2,1)S(1)}, bf16[2,1664,768]{2,1,0:T(8,128)(2,1)}, bf16[2,1664,768]{2,1,0:T(8,128)(2,1)}, bf16[2,1664...) while((s32[]{:T(128)}, ...), condition=%wide.region_7.8_spmd, body=%wide.region_5.7_spmd.sunk | while | flops 1326610944 | bytes 105001104 | solution.py:167
  404.3 3.4 constant_dynamic-slice_fusion.16
  407.9 1.9 constant_dynamic-slice_fusion.18
  409.8 9.4 fusion.133
  419.2 10.3 %fusion.134 = bf16[12,128,1664]{2,1,0:T(8,128)(2,1)} fusion(f32[12,128,1664]{2,1,0:T(8,128)} %get-tuple-element.444, f32[2,12,128,1664]{3,2,1,0:T(8,128)} %get-tuple-element.502, s32[]{:T(128)S(6)} %copy.256, f32[12,128]{1,0:T(8,128)S(1)} %get-tuple-element.445), kind=kLoop, calls=%fused_computation.7.clone.1 | loop fusion | flops 10223616 | bytes 25565188 | tf_op jit(solution)/shard_map/reshape.27
  429.5 5.2 convolution_convert_fusion.11
  434.9 4.9 fusion.135
  439.7 4.5 copy.232
  444.3 4.8 convolution_convert_fusion.12
  449.1 4.5 copy.233
  453.6 5.1 constant_dynamic-update-slice_fusion.9
  458.7 3.4 constant_dynamic-slice_fusion.16
  464.2 9.4 fusion.133
  473.6 10.3 %fusion.134 = bf16[12,128,1664]{2,1,0:T(8,128)(2,1)} fusion(f32[12,128,1664]{2,1,0:T(8,128)} %get-tuple-element.444, f32[2,12,128,1664]{3,2,1,0:T(8,128)} %get-tuple-element.502, s32[]{:T(128)S(6)} %copy.256, f32[12,128]{1,0:T(8,128)S(1)} %get-tuple-element.445), kind=kLoop, calls=%fused_computation.7.clone.1 | loop fusion | flops 10223616 | bytes 25565188 | tf_op jit(solution)/shard_map/reshape.27
  483.9 5.2 convolution_convert_fusion.11
  489.2 4.9 fusion.135
  494.1 4.5 copy.232
  498.7 4.8 convolution_convert_fusion.12
  503.5 4.5 copy.233
  508.0 5.1 constant_dynamic-update-slice_fusion.9
  513.1 2.8 slice.34
  515.9 3.9 fusion.59
  521.1 5.8 add_convert_fusion
  527.0 6.0 broadcast.176
  533.0 15.2 %scatter_fusion = bf16[64,128,768]{2,1,0:T(8,128)(2,1)} fusion(bf16[64,128,768]{2,1,0:T(8,128)(2,1)} %broadcast.176, s32[24]{0:T(128)S(1)} %copy-done.24, bf16[24,128,768]{2,1,0:T(8,128)(2,1)} %bitcast.251), kind=kCustom, calls=%fused_computation.1 | custom fusion | bytes 14155872 | tf_op jit(solution)/shard_map/scatter | solution.py:191
  548.3 23.6 %copy.185 = bf16[1,32,2,128,768]{4,2,3,0,1:T(2,128)(2,1)} copy(bf16[1,32,2,128,768]{4,3,2,1,0:T(8,128)(2,1)} %bitcast.228) | data formatting | bytes 25165824 | tf_op jit(solution)/shard_map/reshape | solution.py:193
  571.9 5.3 all-to-all-start.1
  579.8 1.9 convolution_bitcast_fusion
  581.7 1.9 fusion.62
  583.6 3.0 bitcast_select_fusion
  586.7 4.2 fusion.60
  591.0 1.9 bitcast_add_fusion.1
  592.9 4.2 fusion.61
  597.1 1.9 bitcast_add_fusion
  603.9 308.0 %all-reduce.4.cloned.1.call-done = (f32[768,768]{0,1:T(8,128)}, f32[768,768]{0,1:T(8,128)}, f32[768,768]{0,1:T(8,128)}, f32[768,768]{0,1:T(8,128)}) async-done(((f32[768,768]{0,1:T(8,128)}, f32[768,768]{0,1:T(8,128)}, f32[768,768]{0,1:T(8,128)}, f32[768,768]{0,1:T(8,128)}), (f32[768,768]{0,1:T(8,128)}, f32[768,768]{0,1:T(8,128)}, f32[768,768]{0,1:T(8,128)}, ...) | async-done | bytes 9437200 | tf_op jit(solution)/shard_map/psum | solution.py:205
  911.9 2.0 broadcast_multiply_fusion.3
  913.9 2.0 copy.191
  917.8 2.0 copy.192
  921.6 2.0 copy.193
  925.4 2.0 copy.194
  927.4 11.3 %fusion.37 = bf16[1,8,128,768]{3,1,2,0:T(8,128)(2,1)S(1)} fusion(bf16[1,32,2,128,768]{4,2,3,0,1:T(2,128)(2,1)} %all-to-all-done.1, bf16[32,2,8]{0,2,1:T(8,128)(2,1)S(1)} %copy-done.20), kind=kOutput, calls=%fused_computation.68 | convolution fusion | flops 101449728 | bytes 14156800 | tf_op jit(solution)/shard_map/dcs,bdcnw->bsnw/dot_general | solution.py:199
  (134 shorter events, 27.2 us)
Async XLA Ops:
  7.2 47.4 %copy-start = (bf16[768,768]{1,0:T(8,128)(2,1)S(1)}, bf16[768,768]{1,0:T(8,128)(2,1)}, u32[]{:S(2)}) copy-start(bf16[768,768]{1,0:T(8,128)(2,1)} %param.22) | copy-start | bytes 3538948
  10.7 5.1 copy-start.19
  37.7 10.4 %copy-start.6 = (bf16[1,2,128,768]{3,2,1,0:T(8,128)(2,1)S(1)}, bf16[1,2,128,768]{3,2,1,0:T(8,128)(2,1)}, u32[]{:S(2)}) copy-start(bf16[1,2,128,768]{3,2,1,0:T(8,128)(2,1)} %param.14) | copy-start | bytes 1179652
  37.8 10.4 %copy-start.12 = (bf16[768,768]{1,0:T(8,128)(2,1)S(1)}, bf16[768,768]{1,0:T(8,128)(2,1)}, u32[]{:S(2)}) copy-start(bf16[768,768]{1,0:T(8,128)(2,1)} %param.20) | copy-start | bytes 3538948
  37.8 240.9 %all-to-all-start = ((bf16[1,32,2,128,768]{4,3,2,0,1:T(8,128)(2,1)}), bf16[1,32,2,128,768]{4,3,2,0,1:T(8,128)(2,1)}, u32[]{:S(2)}, u32[]{:S(2)}) async-start(bf16[1,32,2,128,768]{4,3,2,0,1:T(8,128)(2,1)} %copy.171), calls=%async_computation | async-start | bytes 25165824 | tf_op jit(solution)/shard_map/all_to_all | solution.py:124
  50.9 3.6 copy-start.8
  53.5 0.5 copy-start.23
  54.0 0.5 copy-start.21
  286.3 3.4 copy-start.13
  286.3 3.4 copy-start.16
  314.2 6.8 copy-start.10
  314.2 6.8 copy-start.11
  343.8 9.6 %copy-start.1 = (bf16[1,1664,768]{1,2,0:T(8,128)(2,1)S(1)}, bf16[1,1664,768]{1,2,0:T(8,128)(2,1)}, u32[]{:S(2)}) copy-start(bf16[1,1664,768]{1,2,0:T(8,128)(2,1)} %get-tuple-element.428) | copy-start | bytes 7667716 | tf_op jit(solution)/shard_map/while
  380.5 9.6 %copy-start.1 = (bf16[1,1664,768]{1,2,0:T(8,128)(2,1)S(1)}, bf16[1,1664,768]{1,2,0:T(8,128)(2,1)}, u32[]{:S(2)}) copy-start(bf16[1,1664,768]{1,2,0:T(8,128)(2,1)} %get-tuple-element.428) | copy-start | bytes 7667716 | tf_op jit(solution)/shard_map/while
  403.4 0.7 copy-start.4
  513.1 2.8 copy-start.14
  513.1 6.7 slice-start
  515.9 3.9 copy-start.3
  515.9 3.9 slice-start.1
  519.8 1.3 copy-start.17
  520.1 6.8 copy-start.2
  527.0 6.1 copy-start.24
  571.9 7.9 copy-start.7
  571.9 355.5 %all-to-all-start.1 = ((bf16[1,32,2,128,768]{4,2,3,0,1:T(2,128)(2,1)}), bf16[1,32,2,128,768]{4,2,3,0,1:T(2,128)(2,1)}, u32[]{:S(2)}, u32[]{:S(2)}) async-start(bf16[1,32,2,128,768]{4,2,3,0,1:T(2,128)(2,1)} %copy.185), calls=%async_computation.1 | async-start | bytes 25165824 | tf_op jit(solution)/shard_map/all_to_all | solution.py:192
  577.2 4.5 copy-start.5
  577.2 6.5 copy-start.22
  577.2 334.7 %all-reduce.4.cloned.1.call-start = ((), (), s32[]{:S(2)}) async-start(), calls=%async_computation.2 | async-start | bytes 18874368 | tf_op jit(solution)/shard_map/psum | solution.py:205
  577.6 4.1 copy-start.9
  581.7 5.0 slice-start.4
  583.6 3.1 slice-start.5
  583.6 9.3 slice-start.2
  586.7 6.2 slice-start.3
  599.1 3.0 copy-start.15
  599.1 3.5 copy-start.18
  923.5 3.8 copy-start.20
Sparse Core Ops, SparseCore 0:
  599.2 312.6 all-reduce.3
where the time goes:
time: 954 us; the launch traced here: 947 us
  waiting for transfers between devices  532 us (56%)
  local copies, waits for them, and re-layouts  169 us (18%)
  matrix products  135 us (14%)
  other arithmetic  80.4 us (8%)
  starting transfers between devices  16.1 us (2%)
  between operations  14.7 us (2%)
    psum x1, waiting for transfers between devices, body(): lax.psum((grad_wq, grad_wk, grad_wv, grad_wo), ('dp', 'patch'))  308 us
    all_to_all x1, waiting for transfers between devices, body(): lax.all_to_all(outgoing, 'patch', split_axis=1, concat_axis=1, tiled=True)  224 us
    dynamic_update_slice x4, other arithmetic, body(): lax.map(forward_group, (queries, all_keys, all_values, live_row))  36.7 us
    dynamic_update_slice x6, local copies, waits for them, and re-layouts, body(): lax.map(backward_group, (queries, all_keys, all_values, soft_probs, soft_...  28.3 us
    reshape x1, local copies, waits for them, and re-layouts, body(): back_rows.reshape(batch_local, peer_count, capacity, block_rows, model_wi...  23.6 us
    convert_element_type x1, local copies, waits for them, and re-layouts, body(): outgoing = jnp.einsum('dcs,bsnw->bdcnw', chooser, past_tokens, preferred_...  21.9 us
    dynamic_slice x14, local copies, waits for them, and re-layouts, body(): lax.map(forward_group, (queries, all_keys, all_values, live_row))  21.3 us
    another operation x4, other arithmetic  20.6 us
  transfers between devices with their start and end apart: 3, of which 2 were waited for; matrix products, arithmetic and copies ran while one was open for 5% of the time, Pallas kernels for 0%

commit v1 on v0

--- a/solution.py
+++ b/solution.py
@@ -203,7 +203,7 @@
     grad_wk = outer_sum(token_rows, own_k) + outer_sum(fetched_rows, far_k)
     grad_wv = outer_sum(token_rows, own_v) + outer_sum(fetched_rows, far_v)
     grad_wq, grad_wk, grad_wv, grad_wo = lax.psum(
-        (grad_wq, grad_wk, grad_wv, grad_wo), ("dp", "patch")
+        lax.psum((grad_wq, grad_wk, grad_wv, grad_wo), "patch"), "dp"
     )
     inv_total = 1.0 / math.sqrt(
         lax.axis_size("dp") * batch_local * peer_count * patch_local * block_rows

time: 954 us -> 1270 us (1.33)
  waiting for transfers between devices: 532 us -> 845 us
    psum x1 -> x2, waiting for transfers between devices: 308 us -> 620 us  [the longest x1 439 us: body(): lax.psum((grad_wq, grad_wk, grad_wv, grad_wo), 'patch')]
  transfers between devices with their start and end apart: 3 -> 4, of which waited for: 2 -> 3; matrix products, arithmetic and copies ran while one was open for 5% -> 6% of each run, Pallas kernels for 0% -> 0%
where the time goes in v1:
time: 1270 us; the launch traced here: 1260 us
  waiting for transfers between devices  845 us (67%)
  local copies, waits for them, and re-layouts  172 us (14%)
  matrix products  137 us (11%)
  other arithmetic  77.9 us (6%)
  starting transfers between devices  15.2 us (1%)
  between operations  14.9 us (1%)
    psum x1, waiting for transfers between devices, body(): lax.psum((grad_wq, grad_wk, grad_wv, grad_wo), 'patch')  439 us
    all_to_all x1, waiting for transfers between devices, body(): lax.all_to_all(outgoing, 'patch', split_axis=1, concat_axis=1, tiled=True)  224 us
    psum x1, waiting for transfers between devices, body(): lax.psum(lax.psum((grad_wq, grad_wk, grad_wv, grad_wo), 'patch'), 'dp')  181 us
    dynamic_update_slice x4, other arithmetic, body(): lax.map(forward_group, (queries, all_keys, all_values, live_row))  36.7 us
    dynamic_update_slice x6, local copies, waits for them, and re-layouts, body(): lax.map(backward_group, (queries, all_keys, all_values, soft_probs, soft_...  28.4 us
  transfers between devices with their start and end apart: 4, of which 3 were waited for; matrix products, arithmetic and copies ran while one was open for 6% of the time, Pallas kernels for 0%

profile of v1, /device:TPU:1, one launch (start us, length us, event | category | flops | bytes accessed | tf_op | source)
XLA Modules:
  0.0 1262.1 jit_solution(17473348396291262676)
XLA Ops:
  10.7 5.1 convert_bitcast_fusion
  15.9 21.8 %copy.171 = bf16[1,32,2,128,768]{4,3,2,0,1:T(8,128)(2,1)} copy(bf16[1,32,2,128,768]{4,1,3,2,0:T(8,128)(2,1)S(1)} %convert_bitcast_fusion) | data formatting | bytes 25165824 | tf_op jit(solution)/shard_map/convert_element_type | solution.py:123
  37.7 10.0 all-to-all-start
  47.8 2.7 fusion.24
  54.7 224.2 %all-to-all-done = bf16[1,32,2,128,768]{4,3,2,0,1:T(8,128)(2,1)} async-done(((bf16[1,32,2,128,768]{4,3,2,0,1:T(8,128)(2,1)}), bf16[1,32,2,128,768]{4,3,2,0,1:T(8,128)(2,1)}, u32[]{:S(2)}, u32[]{:S(2)}) %all-to-all-start) | async-done | bytes 12582944 | tf_op jit(solution)/shard_map/all_to_all | solution.py:124
  278.9 7.7 gather_fusion
  286.6 3.6 bitcast_select_fusion.1
  290.2 9.8 convolution_convert_fusion.3
  300.0 7.9 fusion.56
  308.0 6.7 copy.173
  314.7 6.8 copy.175
  321.4 8.5 pad_maximum_fusion
  330.0 73.3 %while.28 = (s32[]{:T(128)}, bf16[2,128,768]{2,1,0:T(8,128)(2,1)S(1)}, f32[2,12,128,1664]{3,2,1,0:T(8,128)}, bf16[2,12,128,1664]{3,2,1,0:T(8,128)(2,1)}, bf16[2,...) while((s32[]{:T(128)}, ...), condition=%wide.region_4.5_spmd, body=%wide.region_1.0_spmd.sunk | while | flops 672304384 | bytes 83390360 | solution.py:159
  330.0 5.1 constant_dynamic-slice_fusion.14
  335.2 8.5 fusion.124
  343.7 9.6 bitcast_dynamic-update-slice_fusion.4
  353.3 4.4 convolution_convert_fusion.10
  357.9 8.8 bitcast_dynamic-update-slice_fusion.5
  366.7 5.1 constant_dynamic-slice_fusion.14
  371.9 8.5 fusion.124
  380.4 9.6 bitcast_dynamic-update-slice_fusion.4
  390.0 4.4 convolution_convert_fusion.10
  394.6 8.7 bitcast_dynamic-update-slice_fusion.5
  404.1 109.3 %while.29 = (s32[]{:T(128)}, bf16[2,128,768]{2,1,0:T(8,128)(2,1)S(1)}, bf16[2,1664,768]{2,1,0:T(8,128)(2,1)}, bf16[2,1664,768]{2,1,0:T(8,128)(2,1)}, bf16[2,1664...) while((s32[]{:T(128)}, ...), condition=%wide.region_7.8_spmd, body=%wide.region_5.7_spmd.sunk | while | flops 1326610944 | bytes 105001104 | solution.py:167
  404.5 3.4 constant_dynamic-slice_fusion.16
  408.0 1.9 constant_dynamic-slice_fusion.18
  409.9 9.4 fusion.133
  419.3 10.3 fusion.134
  429.6 5.2 convolution_convert_fusion.11
  435.0 4.8 fusion.135
  439.8 4.6 copy.232
  444.4 4.8 convolution_convert_fusion.12
  449.2 4.5 copy.233
  453.8 5.1 constant_dynamic-update-slice_fusion.9
  458.9 3.4 constant_dynamic-slice_fusion.16
  464.4 9.4 fusion.133
  473.7 10.3 fusion.134
  484.0 5.2 convolution_convert_fusion.11
  489.4 4.8 fusion.135
  494.3 4.6 copy.232
  498.8 4.8 convolution_convert_fusion.12
  503.6 4.5 copy.233
  508.2 5.1 constant_dynamic-update-slice_fusion.9
  514.6 2.8 slice.34
  518.0 3.4 slice-done
  522.7 1.9 convolution_bitcast_fusion
  524.7 4.2 fusion.60
  529.0 4.2 fusion.61
  533.2 1.9 fusion.62
  535.2 1.9 bitcast_add_fusion.1
  537.1 1.9 bitcast_add_fusion
  539.1 6.5 fusion.59
  545.7 5.8 add_convert_fusion
  551.4 6.0 broadcast.176
  557.5 15.3 %scatter_fusion = bf16[64,128,768]{2,1,0:T(8,128)(2,1)} fusion(bf16[64,128,768]{2,1,0:T(8,128)(2,1)} %broadcast.176, s32[24]{0:T(128)S(1)} %copy-done.21, bf16[24,128,768]{2,1,0:T(8,128)(2,1)} %bitcast.251), kind=kCustom, calls=%fused_computation.1 | custom fusion | bytes 14155872 | tf_op jit(solution)/shard_map/scatter | solution.py:191
  572.8 23.7 %copy.185 = bf16[1,32,2,128,768]{4,2,3,0,1:T(2,128)(2,1)} copy(bf16[1,32,2,128,768]{4,3,2,1,0:T(8,128)(2,1)} %bitcast.228) | data formatting | bytes 25165824 | tf_op jit(solution)/shard_map/reshape | solution.py:193
  596.5 5.1 all-to-all-start.1
  601.6 439.0 %all-reduce.6.cloned.1.call-done = (f32[768,768]{0,1:T(8,128)}, f32[768,768]{0,1:T(8,128)}, f32[768,768]{0,1:T(8,128)}, f32[768,768]{0,1:T(8,128)}) async-done(((f32[768,768]{0,1:T(8,128)}, f32[768,768]{0,1:T(8,128)}, f32[768,768]{0,1:T(8,128)}, f32[768,768]{0,1:T(8,128)}), (f32[768,768]{0,1:T(8,128)}, f32[768,768]{0,1:T(8,128)}, f32[768,768]{0,1:T(8,128)}, ...) | async-done | bytes 9437200 | tf_op jit(solution)/shard_map/psum | solution.py:206
  1045.5 11.3 fusion.37
  1058.3 181.3 %all-reduce.8.cloned.1.call-done = (f32[768,768]{0,1:T(8,128)}, f32[768,768]{0,1:T(8,128)}, f32[768,768]{0,1:T(8,128)}, f32[768,768]{0,1:T(8,128)}) async-done(((f32[768,768]{0,1:T(8,128)}, f32[768,768]{0,1:T(8,128)}, f32[768,768]{0,1:T(8,128)}, f32[768,768]{0,1:T(8,128)}), (f32[768,768]{0,1:T(8,128)}, f32[768,768]{0,1:T(8,128)}, f32[768,768]{0,1:T(8,128)}, ...) | async-done | bytes 9437200 | tf_op jit(solution)/shard_map/psum | solution.py:205
  1241.5 2.0 copy.191
  1245.3 2.0 copy.192
  1249.1 2.0 copy.193
  1253.0 2.0 copy.194
  (135 shorter events, 28.3 us)
Async XLA Ops:
  7.2 47.0 %copy-start = (bf16[768,768]{1,0:T(8,128)(2,1)S(1)}, bf16[768,768]{1,0:T(8,128)(2,1)}, u32[]{:S(2)}) copy-start(bf16[768,768]{1,0:T(8,128)(2,1)} %param.22) | copy-start | bytes 3538948
  10.7 5.1 copy-start.18
  37.7 10.1 copy-start.6
  37.7 10.2 copy-start.12
  37.7 241.2 %all-to-all-start = ((bf16[1,32,2,128,768]{4,3,2,0,1:T(8,128)(2,1)}), bf16[1,32,2,128,768]{4,3,2,0,1:T(8,128)(2,1)}, u32[]{:S(2)}, u32[]{:S(2)}) async-start(bf16[1,32,2,128,768]{4,3,2,0,1:T(8,128)(2,1)} %copy.171), calls=%async_computation | async-start | bytes 25165824 | tf_op jit(solution)/shard_map/all_to_all | solution.py:124
  47.7 992.9 %all-reduce.6.cloned.1.call-start = ((), (), s32[]{:S(2)}) async-start(), calls=%async_computation.2 | async-start | bytes 18874368 | tf_op jit(solution)/shard_map/psum | solution.py:206
  50.6 3.6 copy-start.8
  53.1 0.5 copy-start.20
  53.6 0.5 copy-start.22
  286.6 3.6 copy-start.13
  286.6 3.6 copy-start.15
  314.6 6.8 copy-start.10
  314.6 6.8 copy-start.11
  343.7 9.6 copy-start.1
  380.4 9.6 copy-start.1
  403.3 0.7 copy-start.4
  513.4 4.1 slice-start.2
  514.6 3.0 slice-start.3
  517.5 7.2 copy-start.2
  517.6 3.7 slice-start
  517.7 3.8 slice-start.1
  517.7 3.8 copy-start.23
  521.5 7.4 copy-start.3
  521.5 1.3 copy-start.7
  528.9 4.3 copy-start.5
  528.9 4.3 copy-start.9
  539.0 6.6 slice-start.4
  539.1 6.6 slice-start.5
  539.1 6.6 copy-start.16
  551.4 6.0 copy-start.21
  596.5 449.0 %all-to-all-start.1 = ((bf16[1,32,2,128,768]{4,2,3,0,1:T(2,128)(2,1)}), bf16[1,32,2,128,768]{4,2,3,0,1:T(2,128)(2,1)}, u32[]{:S(2)}, u32[]{:S(2)}) async-start(bf16[1,32,2,128,768]{4,2,3,0,1:T(2,128)(2,1)} %copy.185), calls=%async_computation.1 | async-start | bytes 25165824 | tf_op jit(solution)/shard_map/all_to_all | solution.py:192
  601.6 638.0 %all-reduce.8.cloned.1.call-start = ((), (), s32[]{:S(2)}) async-start(), calls=%async_computation.3 | async-start | bytes 18874368 | tf_op jit(solution)/shard_map/psum | solution.py:205
  1040.7 3.0 copy-start.14
  1040.7 3.6 copy-start.17
  1040.7 4.8 copy-start.19
Sparse Core Ops, SparseCore 0:
  539.2 501.4 all-reduce.5
  1043.7 195.9 all-reduce.7
